TPU v7x, 256 devices: a whole 4x4x8 slice. The times are simulated.
256 devices in a mesh: dp: 16 (over z, core), expert: 16 (over x, y).
Axes of the slice: x: 4, y: 4, z: 8, core: 2. Of those that a mesh axis runs over, the one named last changes fastest.
Arguments:
- tokens: bfloat16 [32768, 2048], P(('dp', 'expert')), may hold values from -6 to 6
- expert_ids: int32 [32768, 4], P(('dp', 'expert')), may hold values from 0 to 31, as said below
- gate_weights: float32 [32768, 4], P(('dp', 'expert')), may hold values from 0.1 to 0.6
- hot_ids: int32 [2], replicated, may hold values from 0 to 31, as said below
- w_gate: bfloat16 [32, 2048, 768], P('expert', 'dp'), may hold values from -0.125 to 0.125
- w_up: bfloat16 [32, 2048, 768], P('expert', 'dp'), may hold values from -0.125 to 0.125
- w_down: bfloat16 [32, 768, 2048], P('expert', None, 'dp'), may hold values from -0.21875 to 0.21875
Outputs:
- moe_out: bfloat16 [32768, 2048], P(('dp', 'expert'))
Inputs may be any that keep to these rules, and one draw needn't show every extreme that they name: `expert_ids`: tokens are in aligned blocks of 128 rows, one block a device. Column 0 of each row names an expert of hot_ids, each listed expert exactly 64 times in every block. Columns 1 to 3 name experts outside hot_ids, all different within a row; each such expert appears at most 24 times in a block, and one of them exactly 24 times in every block. `hot_ids`: the listed experts are all different, and one of them is expert 32 - 1.
All inputs are finite; a program needn't handle non-finite values.
Results may differ from a plain program's by a relative error of at most 0.0057.
Values may be sent and summed in bfloat16 or wider, within the bound.
A program may use at most 384 MiB of HBM per device.

v0:
```python
import jax
import jax.numpy as jnp
from jax import lax
from jax.sharding import PartitionSpec as P


def sent_together(arrays, axis, dim, along):
    ends, at = ([], 0)
    for a in arrays[:-1]:
        at += a.shape[along]
        ends.append(at)
    both = jnp.concatenate(arrays, axis=along)
    return tuple(jnp.split(lax.all_gather(both, axis, axis=dim, tiled=True), ends, axis=along))


def capacity(tok_rows, top_k, hot_count, experts):
    return min(tok_rows, max(8, 8 * (2 * tok_rows * (top_k - 1) // ((experts - hot_count) * 8))))


def expert_ffn(token_rows, gate_weight, up_weight, down_weight):
    pieces = sent_together((gate_weight, up_weight), "dp", 1, 0)
    gate_part = jnp.einsum(
        "aecd,edf->aecf", token_rows, pieces[0], preferred_element_type=jnp.float32
    )
    up_part = jnp.einsum(
        "aecd,edf->aecf", token_rows, pieces[1], preferred_element_type=jnp.float32
    )
    hidden = (jax.nn.silu(gate_part) * up_part).astype(jnp.bfloat16)
    return jnp.einsum(
        "aecf,efn->aecn",
        hidden,
        lax.all_gather(down_weight, "dp", axis=2, tiled=True),
        preferred_element_type=jnp.float32,
    ).astype(jnp.bfloat16)


def send_to_owners(
    tokens, pair_ids, pair_gates, per_token, slot_cap, gate_weight, up_weight, down_weight
):
    tok_rows, model_width = tokens.shape
    expert_count = lax.axis_size("expert")
    local_count = gate_weight.shape[0]
    experts = expert_count * local_count
    pair_count = pair_ids.shape[0]
    onehot = (pair_ids[:, None] == jnp.arange(experts, dtype=jnp.int32)[None, :]).astype(jnp.int32)
    rank_index = jnp.sum(jnp.cumsum(onehot, axis=0) * onehot, axis=1) - 1
    slot_index = pair_ids * slot_cap + rank_index
    pair_token = jnp.arange(pair_count, dtype=jnp.int32) // per_token
    slot_table = jnp.full((experts * slot_cap,), tok_rows, jnp.int32).at[slot_index].set(pair_token)
    padded = jnp.concatenate([tokens, jnp.zeros((1, model_width), jnp.bfloat16)], axis=0)
    outgoing = padded[slot_table].reshape(expert_count, local_count, slot_cap, model_width)
    arrived = lax.all_to_all(outgoing, "expert", split_axis=0, concat_axis=0, tiled=True)
    expert_out = expert_ffn(arrived, gate_weight, up_weight, down_weight)
    returned = lax.all_to_all(
        expert_out, "expert", split_axis=0, concat_axis=0, tiled=True
    ).reshape(experts * slot_cap, model_width)
    picked = returned[slot_index].astype(jnp.float32) * pair_gates[:, None]
    return jnp.sum(picked.reshape(tok_rows, per_token, model_width), axis=1)


def shards(tokens, expert_ids, gate_weights, hot_ids, w_gate, w_up, w_down):
    tok_rows, top_k = expert_ids.shape
    hot_count = hot_ids.shape[0]
    local_count = w_gate.shape[0]
    experts = lax.axis_size("expert") * local_count
    cold_cap = capacity(tok_rows, top_k, hot_count, experts)
    hot_cap = tok_rows // hot_count
    output_sum = send_to_owners(
        tokens,
        expert_ids.reshape(tok_rows * top_k),
        gate_weights.reshape(tok_rows * top_k),
        top_k,
        max(cold_cap, hot_cap),
        w_gate,
        w_up,
        w_down,
    )
    return output_sum.astype(jnp.bfloat16)


def solution(mesh):
    placed = (
        P(("dp", "expert"), None),
        P(("dp", "expert"), None),
        P(("dp", "expert"), None),
        P(),
        P("expert", "dp", None),
        P("expert", "dp", None),
        P("expert", None, "dp"),
    )
    return jax.shard_map(
        shards, mesh=mesh, in_specs=placed, out_specs=P(("dp", "expert"), None), check_vma=False
    )
```

profile of v0, /device:TPU:1, one launch (start us, length us, event | category | flops | bytes accessed | tf_op | source)
XLA Modules:
  0.0 354.2 jit_solution(17678732230369086016)
XLA Ops:
  6.5 0.0 all-gather.3.cloned.1.call-start
  6.5 2.1 pad_maximum_fusion
  8.6 0.0 all-gather.3.cloned.1.call-update
  8.6 0.0 all-gather.5.cloned.1.call-start
  8.7 0.7 all-gather.5.cloned.1.call-update
  9.4 0.8 copy.16
  10.2 0.1 eq.29
  10.3 0.1 eq.25
  10.4 0.7 broadcast_multiply_fusion
  11.1 1.2 reduce-window.6
  12.3 0.2 slice_reduce_fusion
  12.5 0.1 copy.15
  12.6 0.1 mul.37
  12.8 0.1 fusion.18
  12.9 1.1 concatenate.7
  14.0 2.5 scatter_custom_fusion
  16.5 11.0 %gather_fusion = bf16[2048,2048]{1,0:T(8,128)(2,1)} fusion(bf16[129,2048]{1,0:T(8,128)(2,1)S(1)} %concatenate.7, s32[2048]{0:T(1024)S(1)} %fusion.20), kind=kCustom, calls=%fused_computation | custom fusion | bytes 16785408 | tf_op jit(solution)/shard_map/gather | solution.py:51
  27.5 102.4 %all_to_all.10 = bf16[16,2,64,2048]{3,2,1,0:T(8,128)(2,1)} all-to-all(bf16[16,2,64,2048]{3,2,1,0:T(8,128)(2,1)} %bitcast.63), channel_id=1, replica_groups=mesh['dp'=16,'expert'=16] {'expert'}, dimensions={0} | all-to-all | bytes 16777216 | tf_op jit(solution)/shard_map/all_to_all | solution.py:52
  129.9 0.0 all-gather.3.cloned.1.call-done
  129.9 12.7 %fusion = f32[2,768,16,64]{1,3,2,0:T(8,128)} fusion(bf16[16,2,64,2048]{3,2,1,0:T(8,128)(2,1)} %all_to_all.10, bf16[4,2048,768]{2,1,0:T(8,128)(2,1)} %all-gather.3.cloned.1.call-done), kind=kOutput, calls=%fused_computation.4 | convolution fusion | flops 6442450944 | bytes 20971520 | tf_op jit(solution)/shard_map/aecd,edf->aecf/dot_general | solution.py:25
  142.6 2.6 all-gather.5.cloned.1.call-done
  145.3 22.3 %convert_bitcast_fusion = bf16[16,2,64,2048]{3,2,0,1:T(8,128)(2,1)} fusion(bf16[2,768,2048]{2,1,0:T(8,128)(2,1)} %all-gather.5.cloned.1.call-done, f32[2,768,16,64]{1,3,2,0:T(8,128)} %fusion, bf16[16,2,64,2048]{3,2,1,0:T(8,128)(2,1)} %all_to_all.10, bf16[4,2048,768]{2,1,0:T(8,128)(2,1)} %all-gather.3.cloned.1.call-done), kind=kOutput, calls=%fused_computation.3 | convolution fusion | flops 12898533376 | bytes 35651584 | tf_op jit(solution)/shard_map/aecf,efn->aecn/dot_general | solution.py:29
  167.6 8.3 %copy.21 = bf16[16,2,64,2048]{3,2,1,0:T(8,128)(2,1)} copy(bf16[16,2,64,2048]{3,2,0,1:T(8,128)(2,1)} %convert_bitcast_fusion) | data formatting | bytes 16777216 | tf_op jit(solution)/shard_map/convert_element_type | solution.py:34
  175.8 0.0 copy-start
  175.8 6.7 %all-to-all-start.1 = ((bf16[16,2,64,2048]{3,2,1,0:T(8,128)(2,1)}), bf16[16,2,64,2048]{3,2,1,0:T(8,128)(2,1)}, u32[]{:S(2)}, u32[]{:S(2)}) async-start(bf16[16,2,64,2048]{3,2,1,0:T(8,128)(2,1)} %copy.21), calls=%async_computation.1 | async-start | bytes 16777216 | tf_op jit(solution)/shard_map/all_to_all | solution.py:54
  182.5 0.0 copy-done
  182.6 0.1 copy.22
  182.7 146.6 %all-to-all-done.1 = bf16[16,2,64,2048]{3,2,1,0:T(8,128)(2,1)} async-done(((bf16[16,2,64,2048]{3,2,1,0:T(8,128)(2,1)}), bf16[16,2,64,2048]{3,2,1,0:T(8,128)(2,1)}, u32[]{:S(2)}, u32[]{:S(2)}) %all-to-all-start.1) | async-done | bytes 8388640 | tf_op jit(solution)/shard_map/all_to_all | solution.py:54
  329.2 8.9 %gather_fusion.1 = bf16[512,2048]{1,0:T(8,128)(2,1)S(1)} fusion(bf16[2048,2048]{1,0:T(8,128)(2,1)} %bitcast.13, s32[1024]{0:T(1024)S(1)} %pad_clamp_fusion), kind=kCustom, calls=%fused_computation.1 | custom fusion | bytes 4196352 | tf_op jit(solution)/shard_map/gather | solution.py:57
  338.1 3.0 reshape.70
  341.2 6.2 %multiply_reduce_fusion = bf16[128,2048]{1,0:T(8,128)(2,1)} fusion(f32[128,4,2048]{2,1,0:T(4,128)} %reshape.70, f32[128,4]{1,0:T(8,128)S(1)} %copy.22), kind=kLoop, calls=%fused_computation.19 | loop fusion | flops 1835008 | bytes 4720640 | tf_op jit(solution)/shard_map/reduce_sum | solution.py:58
  (8 shorter events, 0.1 us)
Async XLA Ops:
  6.5 123.4 %all-gather.3.cloned.1.call-start = ((), (), s32[]{:S(2)}) async-start(), calls=%async_computation.2 | async-start | bytes 13369344 | tf_op jit(solution)/shard_map/all_gather | solution.py:13
  8.6 136.6 %all-gather.5.cloned.1.call-start = ((), (), s32[]{:S(2)}) async-start(), calls=%async_computation.3 | async-start | bytes 6684672 | tf_op jit(solution)/shard_map/all_gather | solution.py:32
  175.8 6.7 %copy-start = (f32[128,4]{0,1:T(4,128)S(1)}, f32[128,4]{0,1:T(4,128)}, u32[]{:S(2)}) copy-start(f32[128,4]{0,1:T(4,128)} %param.9) | copy-start | bytes 6148
  175.8 153.4 %all-to-all-start.1 = ((bf16[16,2,64,2048]{3,2,1,0:T(8,128)(2,1)}), bf16[16,2,64,2048]{3,2,1,0:T(8,128)(2,1)}, u32[]{:S(2)}, u32[]{:S(2)}) async-start(bf16[16,2,64,2048]{3,2,1,0:T(8,128)(2,1)} %copy.21), calls=%async_computation.1 | async-start | bytes 16777216 | tf_op jit(solution)/shard_map/all_to_all | solution.py:54
Sparse Core Ops, SparseCore 0:
  9.2 79.7 all-gather.2
  90.8 54.4 all-gather.4
where the time goes:
time: 359 us; the launch traced here: 354 us
  waiting for transfers between devices  150 us (42%)
  blocking collectives  102 us (28%)
  local copies, waits for them, and re-layouts  36.3 us (10%)
  matrix products  35 us (10%)
  between operations  13.5 us (4%)
  other arithmetic  10.3 us (3%)
  starting transfers between devices  6.76 us (2%)
    all_to_all x1, waiting for transfers between devices, send_to_owners(): lax.all_to_all(expert_out, 'expert', split_axis=0, concat_axis=0, tiled=T...  147 us
    all_to_all x1, blocking collectives, send_to_owners(): lax.all_to_all(outgoing, 'expert', split_axis=0, concat_axis=0, tiled=True)  102 us
    dot_general x1, matrix products, expert_ffn(): jnp.einsum('aecf,efn->aecn', hidden, lax.all_gather(down_weight, 'dp', ax...  22.3 us
    dot_general x1, matrix products, expert_ffn(): jnp.einsum('aecd,edf->aecf', token_rows, pieces[1], preferred_element_typ...  12.7 us
    gather x1, local copies, waits for them, and re-layouts, send_to_owners(): padded[slot_table].reshape(expert_count, local_count, slot_cap, model_width)  11 us
    gather x1, local copies, waits for them, and re-layouts, send_to_owners(): picked = returned[slot_index].astype(jnp.float32) * pair_gates[:, None]  8.86 us
    convert_element_type x1, local copies, waits for them, and re-layouts, expert_ffn(): return jnp.einsum('aecf,efn->aecn', hidden, lax.all_gather(down_weight, '...  8.26 us
  transfers between devices with their start and end apart: 3, of which 2 were waited for; matrix products, arithmetic and copies ran while one was open for 9% of the time, Pallas kernels for 0%

commit v1 on v0

v1 whole, which is shorter than its diff:
```python
import jax
import jax.numpy as jnp
from jax import lax
from jax.experimental import pallas as pl
from jax.experimental.pallas import tpu as pltpu
from jax.sharding import PartitionSpec as P

MESH = pl.DeviceIdType.MESH
NZ = 8
SIDE = 4
SLOTS = 64
DIRS = (1, -1)
F32 = jnp.float32
BF16 = jnp.bfloat16


def kernel(
    tok_in, meta_in, wg_in, wu_in, wd_in, out_ref,
    tok, meta, wgu, wd, xs, hid, gs, pt, ybuf, part, r1, r2, r3, r4, outv,
    lsem, zs, zr, ps, pr, ts, tr, ms, mr, qs, qr, osem,
):
    dp = lax.axis_index("dp")
    ex = lax.axis_index("expert")
    z, k = dp // 2, dp % 2
    x, y = ex // SIDE, ex % SIDE

    def zdev(d):
        return (((z + d + NZ) % NZ) * 2 + k, ex)

    def xdev(d):
        return (dp, ((x + d + SIDE) % SIDE) * SIDE + y)

    def ydev(d):
        return (dp, x * SIDE + (y + d + SIDE) % SIDE)

    partner = (z * 2 + 1 - k, ex)

    def nbr(o, stage, d):
        return xdev(d) if (o + stage) % 2 == 0 else ydev(d)

    barrier = pltpu.get_barrier_semaphore()
    around = [zdev(1), zdev(-1), xdev(1), xdev(-1), ydev(1), ydev(-1), partner]
    for dev in around:
        pl.semaphore_signal(barrier, inc=1, device_id=dev, device_id_type=MESH)

    def zpiece(g, half, zz, core):
        if g < 2:
            rows = pl.multiple_of((zz * 2 + core) * 128, 128)
            return wgu.at[g, pl.ds(rows, 128), pl.ds(half * 768, 768)]
        cols = pl.multiple_of(core * 128, 128)
        return wd.at[zz, half, :, pl.ds(cols, 128)]

    local = []
    for g in range(2):
        for half, src in ((0, wg_in), (1, wu_in)):
            local.append((src.at[g], zpiece(g, half, z, k)))
    for half in range(2):
        local.append((wd_in.at[half], zpiece(2, half, z, k)))
    local.append((tok_in, tok.at[x, y]))
    local.append((meta_in, meta.at[x, y]))
    local = [pltpu.make_async_copy(s, d, lsem.at[i]) for i, (s, d) in enumerate(local)]
    for c in local:
        c.start()
    pl.semaphore_wait(barrier, len(around))
    for c in local:
        c.wait()

    sends = []

    def remote(src, dst, ssem, rsem, dev):
        return pltpu.make_async_remote_copy(
            src_ref=src, dst_ref=dst, send_sem=ssem, recv_sem=rsem,
            device_id=dev, device_id_type=MESH,
        )

    def start(*a):
        c = remote(*a)
        c.start()
        sends.append(c)

    def zsend(g, half, hop, di):
        d = DIRS[di]
        piece = zpiece(g, half, (z - d * (hop - 1) + NZ) % NZ, k)
        n = g * 7 + ((hop - 1) * 2 + half if hop < 4 else 6)
        start(piece, piece, zs.at[di, n], zr.at[di, n], zdev(d))

    def psend(g, half, zz, i):
        piece = zpiece(g, half, zz, k)
        start(piece, piece, ps.at[g, i], pr.at[g, i], partner)

    def own(g):
        for half in range(2):
            for di in range(2):
                zsend(g, half, 1, di)
        for half in range(2):
            psend(g, half, z, half)

    def pump(n):
        g, r = n // 7, n % 7
        for di in range(2):
            d = DIRS[di]
            hop, half = (r // 2 + 1, r % 2) if r < 6 else (4, di)
            zz = (z - d * hop + NZ) % NZ
            piece = zpiece(g, half, zz, k)
            remote(piece, piece, zs.at[di, n], zr.at[di, n], zdev(d)).wait_recv()
            if hop < 3 or (hop == 3 and half == di):
                zsend(g, half, hop + 1, di)
            psend(g, half, zz, 2 + di * 7 + r)
        if r == 5 and g < 2:
            own(g + 1)

    def pwait(g):
        for half in range(2):
            piece = zpiece(g, half, z, 1 - k)
            remote(piece, piece, ps.at[g, half], pr.at[g, half], partner).wait_recv()
        for r in range(7):
            for di in range(2):
                hop, half = (r // 2 + 1, r % 2) if r < 6 else (4, di)
                piece = zpiece(g, half, (z - DIRS[di] * hop + NZ) % NZ, 1 - k)
                i = 2 + di * 7 + r
                remote(piece, piece, ps.at[g, i], pr.at[g, i], partner).wait_recv()

    def major(o):
        return (x, y) if o == 0 else (y, x)

    def half_rows(di):
        return pl.ds(di * 64, 64)

    every = pl.ds(0, 128)

    def tblk(o, mi, rows):
        n = major(o)[1]
        cols = pl.ds(o * 1024, 1024)
        return tok.at[mi, n, rows, cols] if o == 0 else tok.at[n, mi, rows, cols]

    def tcol(o, ni, rows):
        cols = pl.ds(o * 1024, 1024)
        return tok.at[:, ni, rows, cols] if o == 0 else tok.at[ni, :, rows, cols]

    def w4(v):
        return (v + SIDE) % SIDE

    def tok_step(step):
        for o in range(2):
            m, n = major(o)
            for di in range(2):
                d = DIRS[di]

                def got(s, ref):
                    remote(ref, ref, ts.at[s, o, di], tr.at[s, o, di], nbr(o, s // 2, d)).wait_recv()

                if step == 1:
                    got(0, tblk(o, w4(m - d), every))
                    ref = tblk(o, w4(m - d), half_rows(di))
                elif step == 2:
                    got(1, tblk(o, w4(m - 2 * d), half_rows(di)))
                elif step == 3:
                    got(2, tcol(o, w4(n - d), every))
                    ref = tcol(o, w4(n - d), half_rows(di))
                elif step == 4:
                    got(3, tcol(o, w4(n - 2 * d), half_rows(di)))
                if step in (1, 3):
                    start(ref, ref, ts.at[step, o, di], tr.at[step, o, di], nbr(o, step // 2, d))
            if step in (0, 2):
                ref = tblk(o, m, every) if step == 0 else tcol(o, n, every)
                for di in range(2):
                    start(ref, ref, ts.at[step, o, di], tr.at[step, o, di], nbr(o, step // 2, DIRS[di]))

    def meta_step(step):
        def go(i, ref, dev):
            start(ref, ref, ms.at[i], mr.at[i], dev)

        def got(i, ref, dev):
            remote(ref, ref, ms.at[i], mr.at[i], dev).wait_recv()

        if step == 0:
            go(0, meta.at[x, y], xdev(1))
            go(1, meta.at[x, y], xdev(-1))
        elif step == 1:
            got(0, meta.at[w4(x - 1), y], xdev(1))
            go(2, meta.at[w4(x - 1), y], xdev(1))
            got(1, meta.at[w4(x + 1), y], xdev(-1))
        elif step == 2:
            got(2, meta.at[w4(x - 2), y], xdev(1))
            go(3, meta.at[:, y], ydev(1))
            go(4, meta.at[:, y], ydev(-1))
        elif step == 3:
            got(3, meta.at[:, w4(y - 1)], ydev(1))
            go(5, meta.at[:, w4(y - 1)], ydev(1))
            got(4, meta.at[:, w4(y + 1)], ydev(-1))
        else:
            got(5, meta.at[:, w4(y - 2)], ydev(1))

    own(0)
    tok_step(0)
    meta_step(0)
    pump(0)
    meta_step(1)
    tok_step(1)
    pump(1)
    meta_step(2)
    tok_step(2)
    for n in range(2, 8):
        pump(n)
        if n == 3:
            meta_step(3)
        if n == 5:
            meta_step(4)
    tok_step(3)
    for n in range(8, 11):
        pump(n)

    rows = meta[...].reshape(16, 8, 128)
    mine = [(ex * 2).astype(F32), (ex * 2 + 1).astype(F32)]
    hits, gates = [], []
    for e in range(2):
        same = [rows[:, j, :] == mine[e] for j in range(4)]
        hits.append(sum(jnp.where(s, 1.0, 0.0) for s in same))
        gates.append(sum(jnp.where(s, rows[:, 4 + j, :], 0.0) for j, s in enumerate(same)))
    hit = jnp.concatenate(hits, axis=0)
    before = lax.broadcasted_iota(jnp.int32, (128, 128), 0) < lax.broadcasted_iota(jnp.int32, (128, 128), 1)
    rank = jnp.dot(hit.astype(BF16), jnp.where(before, 1.0, 0.0).astype(BF16), preferred_element_type=F32)
    lift = jnp.where(lax.broadcasted_iota(jnp.int32, (32, 128), 0) < 16, 0.0, float(SLOTS))
    slot = jnp.where(hit > 0.5, rank + lift, -1.0)
    slot_cols = jnp.transpose(jnp.concatenate([slot, jnp.zeros((96, 128), F32)], axis=0))

    tok_step(4)
    down_i = lax.broadcasted_iota(jnp.int32, (128, 128), 0).astype(F32)
    across_i = lax.broadcasted_iota(jnp.int32, (128, 128), 1).astype(F32)
    for s in range(16):
        pick = (slot[s:s + 1] == down_i) | (slot[16 + s:17 + s] == down_i)
        gate_of = jnp.where(down_i < SLOTS, gates[0][s:s + 1], gates[1][s:s + 1])
        g_col = jnp.sum(jnp.where(pick, gate_of, 0.0), axis=1, keepdims=True)
        for e in range(2):
            gs[e, pl.ds(s * SLOTS, SLOTS), :] = g_col[e * SLOTS:(e + 1) * SLOTS]
        back = (slot_cols[:, s:s + 1] == across_i) | (slot_cols[:, 16 + s:17 + s] == across_i)
        pt[s] = jnp.where(back, 1.0, 0.0).astype(BF16)
        picked = jnp.where(pick, 1.0, 0.0).astype(BF16)
        got = jnp.dot(picked, tok[s // SIDE, s % SIDE], preferred_element_type=F32).astype(BF16)
        for e in range(2):
            xs[e, pl.ds(s * SLOTS, SLOTS), :] = got[e * SLOTS:(e + 1) * SLOTS]
        if s % 8 == 3:
            pump(11 + s // 8)

    pwait(0)

    def gate_up(e, lo, hi):
        def body(i, carry):
            r0 = pl.multiple_of((i // 3) * 512, 512)
            c0 = pl.multiple_of((i % 3) * 256, 256)
            c1 = pl.multiple_of(768 + (i % 3) * 256, 256)
            rws = xs[e, pl.ds(r0, 512), :]
            gate = jnp.dot(rws, wgu[e, :, pl.ds(c0, 256)], preferred_element_type=F32)
            up = jnp.dot(rws, wgu[e, :, pl.ds(c1, 256)], preferred_element_type=F32)
            h = gate / (1.0 + jnp.exp(-gate)) * up * gs[e, pl.ds(r0, 512), :]
            hid[e, pl.ds(r0, 512), pl.ds(c0, 256)] = h.astype(BF16)
            return carry

        lax.fori_loop(lo, hi, body, 0)

    gate_up(0, 0, 3)
    pump(13)
    gate_up(0, 3, 6)
    pump(14)
    pwait(1)
    gate_up(1, 0, 3)
    pump(15)
    pump(16)
    gate_up(1, 3, 6)
    for n in range(17, 21):
        pump(n)
    pwait(2)

    def cc(o):
        return pl.ds(o * 128, 128)

    def pblk(o, c, mi, rws):
        return part.at[c, mi, :, rws, cc(o)] if o == 0 else part.at[c, :, mi, rws, cc(o)]

    def qblk(o, c, ni, rws):
        return part.at[c, x, ni, rws, cc(o)] if o == 0 else part.at[c, ni, y, rws, cc(o)]

    def link(step, c, o, di):
        m, n = major(o)
        d = DIRS[di]
        if step == 0:
            src, dst = pblk(o, c, w4(m + 2), half_rows(di)), r1.at[c, o, di]
        elif step == 1:
            src, dst = pblk(o, c, w4(m + d), every), r2.at[c, o, di]
        elif step == 2:
            src, dst = qblk(o, c, w4(n + 2), half_rows(di)), r3.at[c, o, di]
        else:
            src, dst = qblk(o, c, w4(n + d), every), r4.at[c, o, di]
        return remote(src, dst, qs.at[step, c, o, di], qr.at[step, c, o, di], nbr(o, step // 2, d))

    def both(fn):
        for o in range(2):
            for di in range(2):
                fn(o, di)

    def plus(ref, *more):
        total = ref[...].astype(F32)
        for v in more:
            total = total + v.astype(F32)
        ref[...] = total.astype(BF16)

    def chunk(c):
        zz = (z + c) % NZ
        for e in range(2):
            yv = jnp.dot(hid[e], wd[zz, e], preferred_element_type=F32).astype(BF16)
            ybuf[:, pl.ds(e * SLOTS, SLOTS), :] = yv.reshape(16, SLOTS, 256)

        def scatter(s, carry):
            v = jnp.dot(pt[s], ybuf[s], preferred_element_type=F32).astype(BF16)
            part[c, s // SIDE, s % SIDE] = v
            return carry

        lax.fori_loop(0, 16, scatter, 0, unroll=4)
        both(lambda o, di: link(0, c, o, di).start())

    def step2(c):
        def one(o, di):
            link(0, c, o, di).wait_recv()
            m = major(o)[0]
            plus(pblk(o, c, w4(m + DIRS[di]), half_rows(di)), r1[c, o, di])
            link(1, c, o, di).start()

        both(one)

    def step3(c):
        for o in range(2):
            for di in range(2):
                link(1, c, o, di).wait_recv()
            plus(pblk(o, c, major(o)[0], every), r2[c, o, 0], r2[c, o, 1])
            for di in range(2):
                link(2, c, o, di).start()

    def step4(c):
        def one(o, di):
            link(2, c, o, di).wait_recv()
            n = major(o)[1]
            plus(qblk(o, c, w4(n + DIRS[di]), half_rows(di)), r3[c, o, di])
            link(3, c, o, di).start()

        both(one)

    def step5(c):
        zz = (z + c) % NZ
        for o in range(2):
            for di in range(2):
                link(3, c, o, di).wait_recv()
            n = major(o)[1]
            total = qblk(o, c, n, every)[...].astype(F32) + r4[c, o, 0].astype(F32) + r4[c, o, 1].astype(F32)
            col = pl.multiple_of(zz * 256 + o * 128, 128)
            outv[:, pl.ds(col, 128)] = total.astype(BF16)

    stages = (chunk, step2, step3, step4, step5)

    def turn(i, carry):
        for j, fn in enumerate(stages):
            @pl.when((i >= j) & (i < NZ + j))
            def _(j=j, fn=fn):
                fn(i - j)
        return carry

    lax.fori_loop(0, NZ + len(stages) - 1, turn, 0)

    final = pltpu.make_async_copy(outv, out_ref, osem)
    final.start()
    for c in sends:
        c.wait_send()

    def drain(c, carry):
        for step in range(4):
            both(lambda o, di: link(step, c, o, di).wait_send())
        return carry

    lax.fori_loop(0, NZ, drain, 0)
    final.wait()


def layer(tokens, expert_ids, gate_weights, hot_ids, w_gate, w_up, w_down):
    meta = jnp.concatenate([expert_ids.astype(F32), gate_weights], axis=1).T
    dma = pltpu.SemaphoreType.DMA
    any_spec = pl.BlockSpec(memory_space=pl.ANY)
    return pl.pallas_call(
        kernel,
        out_shape=jax.ShapeDtypeStruct((128, 2048), BF16),
        in_specs=[any_spec] * 5,
        out_specs=any_spec,
        scratch_shapes=[
            pltpu.VMEM((4, 4, 128, 2048), BF16),
            pltpu.VMEM((4, 4, 8, 128), F32),
            pltpu.VMEM((2, 2048, 1536), BF16),
            pltpu.VMEM((8, 2, 768, 256), BF16),
            pltpu.VMEM((2, 1024, 2048), BF16),
            pltpu.VMEM((2, 1024, 768), BF16),
            pltpu.VMEM((2, 1024, 1), F32),
            pltpu.VMEM((16, 128, 128), BF16),
            pltpu.VMEM((16, 128, 256), BF16),
            pltpu.VMEM((8, 4, 4, 128, 256), BF16),
            pltpu.VMEM((8, 2, 2, 4, 64, 128), BF16),
            pltpu.VMEM((8, 2, 2, 4, 128, 128), BF16),
            pltpu.VMEM((8, 2, 2, 64, 128), BF16),
            pltpu.VMEM((8, 2, 2, 128, 128), BF16),
            pltpu.VMEM((128, 2048), BF16),
            dma((8,)),
            dma((2, 21)), dma((2, 21)),
            dma((3, 16)), dma((3, 16)),
            dma((4, 2, 2)), dma((4, 2, 2)),
            dma((6,)), dma((6,)),
            dma((4, 8, 2, 2)), dma((4, 8, 2, 2)),
            dma,
        ],
        compiler_params=pltpu.CompilerParams(
            collective_id=0, has_side_effects=True, vmem_limit_bytes=67043328
        ),
    )(tokens, meta, w_gate, w_up, w_down)


def solution(mesh):
    placed = (
        P(("dp", "expert"), None),
        P(("dp", "expert"), None),
        P(("dp", "expert"), None),
        P(),
        P("expert", "dp", None),
        P("expert", "dp", None),
        P("expert", None, "dp"),
    )
    return jax.shard_map(
        layer, mesh=mesh, in_specs=placed, out_specs=P(("dp", "expert"), None), check_vma=False
    )
```

time: 359 us -> 162 us (0.45); the launches traced: 354 us -> 162 us
  Pallas kernels: 0 us -> 158 us
  waiting for transfers between devices: 150 us -> 0 us
  blocking collectives: 102 us -> 0 us
  matrix products: 35 us -> 0 us
  local copies, waits for them, and re-layouts: 36.3 us -> 1.89 us
  between operations: 13.5 us -> 0.01 us
  other arithmetic: 10.3 us -> 1.3 us
  starting transfers between devices: 6.76 us -> 0 us
    pallas_call x0 -> x1, Pallas kernels: none -> 158 us  [layer(): pl.pallas_call(kernel, out_shape=jax.ShapeDtypeStruct((128, 2048), BF16),...]
    all_to_all x1 -> x0, waiting for transfers between devices: 147 us -> none  [send_to_owners(): lax.all_to_all(expert_out, 'expert', split_axis=0, concat_axis=0, tiled=T...]
    all_to_all x1 -> x0, blocking collectives: 102 us -> none  [send_to_owners(): lax.all_to_all(outgoing, 'expert', split_axis=0, concat_axis=0, tiled=True)]
    dot_general x2 -> x0, matrix products: 35 us -> none  [the longest x1 22.3 us: expert_ffn(): jnp.einsum('aecf,efn->aecn', hidden, lax.all_gather(down_weight, 'dp', ax...]
    gather x2 -> x0, local copies, waits for them, and re-layouts: 19.9 us -> none  [the longest x1 11 us: send_to_owners(): padded[slot_table].reshape(expert_count, local_count, slot_cap, model_width)]
    convert_element_type x2 -> x0, local copies, waits for them, and re-layouts: 11.3 us -> none  [the longest x1 8.26 us: expert_ffn(): return jnp.einsum('aecf,efn->aecn', hidden, lax.all_gather(down_weight, '...]
    all_to_all x1 -> x0, starting transfers between devices: 6.71 us -> none  [send_to_owners(): lax.all_to_all(expert_out, 'expert', split_axis=0, concat_axis=0, tiled=T...]
    reduce_sum x2 -> x0, other arithmetic: 6.3 us -> none  [the longest x1 6.2 us: send_to_owners(): return jnp.sum(picked.reshape(tok_rows, per_token, model_width), axis=1)]
  transfers between devices with their start and end apart: 3 -> 0, of which waited for: 2 -> 0; matrix products, arithmetic and copies ran while one was open for 9% -> 0% of each run, Pallas kernels for 0% -> 0%
where the time goes in v1:
time: 162 us
  Pallas kernels  158 us (98%)
  local copies, waits for them, and re-layouts  1.89 us (1%)
    pallas_call x1, Pallas kernels, layer(): pl.pallas_call(kernel, out_shape=jax.ShapeDtypeStruct((128, 2048), BF16),...  158 us

profile of v1, /device:TPU:1, one launch (start us, length us, event | category | flops | bytes accessed | tf_op | source)
XLA Modules:
  0.0 161.6 jit_solution(243476937411036548)
XLA Ops:
  0.0 0.0 copy-start
  0.0 0.7 convert_element_type.3
  0.7 0.0 copy-done
  0.7 0.6 maximum_bitcast_fusion.meta_in
  1.3 158.5 %shard_map.64 = bf16[128,2048]{1,0:T(8,128)(2,1)} custom-call(bf16[128,2048]{1,0:T(8,128)(2,1)} %tok_in.1, f32[8,128]{1,0:T(8,128)} %maximum_bitcast_fusion.meta_in, bf16[2,128,768]{2,1,0:T(8,128)(2,1)} %wg_in.1, bf16[2,128,768]{2,1,0:T(8,128)(2,1)} %wu_in.1, bf16[2,768,128]{2,1,0:T(8,128)(2,1)} %wd_in.1), custom_call_target="tpu_custom_call" | custom-call | tf_op jit(solution)/shard_map/pallas_call | solution.py:386
  159.8 1.9 %copy.8 = bf16[128,2048]{1,0:T(8,128)(2,1)} copy(bf16[128,2048]{1,0:T(8,128)(2,1)} %shard_map.64) | data formatting | bytes 1048576
Async XLA Ops:
  0.0 0.7 copy-start

commit v2 on v1

--- a/solution.py
+++ b/solution.py
@@ -15,8 +15,8 @@
 
 
 def kernel(
-    tok_in, meta_in, wg_in, wu_in, wd_in, out_ref,
-    tok, meta, wgu, wd, xs, hid, gs, pt, ybuf, part, r1, r2, r3, r4, outv,
+    tok_in, ids_in, gw_in, wg_in, wu_in, wd_in, out_ref,
+    tok, meta, ids, gw, wgu, wd, acc, hid, gs, pt, ybuf, part, r1, r2, r3, r4, outv,
     lsem, zs, zr, ps, pr, ts, tr, ms, mr, qs, qr, osem,
 ):
     dp = lax.axis_index("dp")
@@ -57,12 +57,17 @@
     for half in range(2):
         local.append((wd_in.at[half], zpiece(2, half, z, k)))
     local.append((tok_in, tok.at[x, y]))
-    local.append((meta_in, meta.at[x, y]))
+    local.append((ids_in, ids))
+    local.append((gw_in, gw))
     local = [pltpu.make_async_copy(s, d, lsem.at[i]) for i, (s, d) in enumerate(local)]
     for c in local:
         c.start()
+    for c in local[-2:]:
+        c.wait()
+    meta[x, y, pl.ds(0, 4)] = ids[...].astype(F32)
+    meta[x, y, pl.ds(4, 4)] = gw[...]
     pl.semaphore_wait(barrier, len(around))
-    for c in local:
+    for c in local[:-2]:
         c.wait()
 
     sends = []
@@ -78,47 +83,61 @@
         c.start()
         sends.append(c)
 
-    def zsend(g, half, hop, di):
+    def arrival(di, r):
+        return (r // 2 + 1, r % 2) if r < 6 else (4, di)
+
+    def zdesc(g, half, hop, di):
         d = DIRS[di]
         piece = zpiece(g, half, (z - d * (hop - 1) + NZ) % NZ, k)
         n = g * 7 + ((hop - 1) * 2 + half if hop < 4 else 6)
-        start(piece, piece, zs.at[di, n], zr.at[di, n], zdev(d))
-
-    def psend(g, half, zz, i):
-        piece = zpiece(g, half, zz, k)
-        start(piece, piece, ps.at[g, i], pr.at[g, i], partner)
+        return remote(piece, piece, zs.at[di, n], zr.at[di, n], zdev(d))
+
+    def pdesc(g, half, zz, i, core):
+        piece = zpiece(g, half, zz, core)
+        return remote(piece, piece, ps.at[g, i], pr.at[g, i], partner)
+
+    def parrival(g, di, r, core):
+        hop, half = arrival(di, r)
+        return pdesc(g, half, (z - DIRS[di] * hop + NZ) % NZ, 2 + di * 7 + r, core)
 
     def own(g):
         for half in range(2):
             for di in range(2):
-                zsend(g, half, 1, di)
+                zdesc(g, half, 1, di).start()
         for half in range(2):
-            psend(g, half, z, half)
+            pdesc(g, half, z, half, k).start()
 
     def pump(n):
         g, r = n // 7, n % 7
         for di in range(2):
             d = DIRS[di]
-            hop, half = (r // 2 + 1, r % 2) if r < 6 else (4, di)
-            zz = (z - d * hop + NZ) % NZ
-            piece = zpiece(g, half, zz, k)
+            hop, half = arrival(di, r)
+            piece = zpiece(g, half, (z - d * hop + NZ) % NZ, k)
             remote(piece, piece, zs.at[di, n], zr.at[di, n], zdev(d)).wait_recv()
             if hop < 3 or (hop == 3 and half == di):
-                zsend(g, half, hop + 1, di)
-            psend(g, half, zz, 2 + di * 7 + r)
+                zdesc(g, half, hop + 1, di).start()
+            parrival(g, di, r, k).start()
         if r == 5 and g < 2:
             own(g + 1)
 
-    def pwait(g):
+    def pwait_own(g):
         for half in range(2):
-            piece = zpiece(g, half, z, 1 - k)
-            remote(piece, piece, ps.at[g, half], pr.at[g, half], partner).wait_recv()
-        for r in range(7):
-            for di in range(2):
-                hop, half = (r // 2 + 1, r % 2) if r < 6 else (4, di)
-                piece = zpiece(g, half, (z - DIRS[di] * hop + NZ) % NZ, 1 - k)
-                i = 2 + di * 7 + r
-                remote(piece, piece, ps.at[g, i], pr.at[g, i], partner).wait_recv()
+            pdesc(g, half, z, half, 1 - k).wait_recv()
+
+    def pwait(g, rs, dis=(0, 1)):
+        for r in rs:
+            for di in dis:
+                parrival(g, di, r, 1 - k).wait_recv()
+
+    def zdrain():
+        for g in range(3):
+            for half in range(2):
+                pdesc(g, half, z, half, k).wait_send()
+            for r in range(7):
+                for di in range(2):
+                    hop, half = arrival(di, r)
+                    zdesc(g, half, hop, di).wait_send()
+                    parrival(g, di, r, k).wait_send()
 
     def major(o):
         return (x, y) if o == 0 else (y, x)
@@ -207,7 +226,7 @@
         if n == 5:
             meta_step(4)
     tok_step(3)
-    for n in range(8, 11):
+    for n in range(8, 10):
         pump(n)
 
     rows = meta[...].reshape(16, 8, 128)
@@ -225,6 +244,8 @@
     slot_cols = jnp.transpose(jnp.concatenate([slot, jnp.zeros((96, 128), F32)], axis=0))
 
     tok_step(4)
+    for c in sends:
+        c.wait_send()
     down_i = lax.broadcasted_iota(jnp.int32, (128, 128), 0).astype(F32)
     across_i = lax.broadcasted_iota(jnp.int32, (128, 128), 1).astype(F32)
     for s in range(16):
@@ -236,40 +257,61 @@
         back = (slot_cols[:, s:s + 1] == across_i) | (slot_cols[:, 16 + s:17 + s] == across_i)
         pt[s] = jnp.where(back, 1.0, 0.0).astype(BF16)
         picked = jnp.where(pick, 1.0, 0.0).astype(BF16)
-        got = jnp.dot(picked, tok[s // SIDE, s % SIDE], preferred_element_type=F32).astype(BF16)
-        for e in range(2):
-            xs[e, pl.ds(s * SLOTS, SLOTS), :] = got[e * SLOTS:(e + 1) * SLOTS]
-        if s % 8 == 3:
-            pump(11 + s // 8)
-
-    pwait(0)
-
-    def gate_up(e, lo, hi):
+        got = jnp.dot(picked, tok[s // SIDE, s % SIDE], preferred_element_type=F32)
+        tok[s // SIDE, s % SIDE] = got.astype(BF16)
+    pump(10)
+    pwait_own(0)
+    pwait(0, range(7))
+
+    def finish(e, gate, up, r0, c0):
+        h = gate / (1.0 + jnp.exp(-gate)) * up * gs[e, pl.ds(r0, 512), :]
+        hid[e, pl.ds(r0, 512), pl.ds(c0, 256)] = h.astype(BF16)
+
+    def gate_up(e, offs, first, last, lo, hi):
         def body(i, carry):
-            r0 = pl.multiple_of((i // 3) * 512, 512)
+            mb = i // 3
+            r0 = pl.multiple_of(mb * 512, 512)
             c0 = pl.multiple_of((i % 3) * 256, 256)
             c1 = pl.multiple_of(768 + (i % 3) * 256, 256)
-            rws = xs[e, pl.ds(r0, 512), :]
-            gate = jnp.dot(rws, wgu[e, :, pl.ds(c0, 256)], preferred_element_type=F32)
-            up = jnp.dot(rws, wgu[e, :, pl.ds(c1, 256)], preferred_element_type=F32)
-            h = gate / (1.0 + jnp.exp(-gate)) * up * gs[e, pl.ds(r0, 512), :]
-            hid[e, pl.ds(r0, 512), pl.ds(c0, 256)] = h.astype(BF16)
+            who = (pl.ds(mb * 2, 2), slice(None), pl.ds(e * SLOTS, SLOTS))
+            sums = [None, None]
+            if offs is None:
+                rws = tok[who + (slice(None),)].reshape(512, 2048)
+                for j, c in enumerate((c0, c1)):
+                    sums[j] = jnp.dot(rws, wgu[e, :, pl.ds(c, 256)], preferred_element_type=F32)
+            else:
+                for j, c in enumerate((c0, c1)):
+                    total = None if first else acc[pl.ds(r0, 512), pl.ds(c, 256)]
+                    for off in offs:
+                        deep = pl.ds(pl.multiple_of(((z + off + NZ) % NZ) * 256, 256), 256)
+                        rws = tok[who + (deep,)].reshape(512, 256)
+                        term = jnp.dot(rws, wgu[e, deep, pl.ds(c, 256)], preferred_element_type=F32)
+                        total = term if total is None else total + term
+                    sums[j] = total
+            if last:
+                finish(e, sums[0], sums[1], r0, c0)
+            else:
+                for j, c in enumerate((c0, c1)):
+                    acc[pl.ds(r0, 512), pl.ds(c, 256)] = sums[j]
             return carry
 
         lax.fori_loop(lo, hi, body, 0)
 
-    gate_up(0, 0, 3)
+    gate_up(0, None, True, True, 0, 4)
+    pump(11)
+    gate_up(0, None, True, True, 4, 6)
+    pwait_own(1)
+    pwait(1, range(4))
+    gate_up(1, (0, -1, 1, -2, 2), True, False, 0, 2)
+    pump(12)
+    gate_up(1, (0, -1, 1, -2, 2), True, False, 2, 6)
+    pwait(1, (4, 5))
+    gate_up(1, (-3, 3), False, False, 0, 6)
     pump(13)
-    gate_up(0, 3, 6)
+    pwait(1, (6,))
+    gate_up(1, (4,), False, True, 0, 6)
     pump(14)
-    pwait(1)
-    gate_up(1, 0, 3)
-    pump(15)
-    pump(16)
-    gate_up(1, 3, 6)
-    for n in range(17, 21):
-        pump(n)
-    pwait(2)
+    pwait_own(2)
 
     def cc(o):
         return pl.ds(o * 128, 128)
@@ -304,8 +346,12 @@
             total = total + v.astype(F32)
         ref[...] = total.astype(BF16)
 
+    def origin(c):
+        near = (c + 1) // 2
+        return (z + NZ + jnp.where(c % 2 == 1, -near, near)) % NZ
+
     def chunk(c):
-        zz = (z + c) % NZ
+        zz = origin(c)
         for e in range(2):
             yv = jnp.dot(hid[e], wd[zz, e], preferred_element_type=F32).astype(BF16)
             ybuf[:, pl.ds(e * SLOTS, SLOTS), :] = yv.reshape(16, SLOTS, 256)
@@ -345,7 +391,7 @@
         both(one)
 
     def step5(c):
-        zz = (z + c) % NZ
+        zz = origin(c)
         for o in range(2):
             for di in range(2):
                 link(3, c, o, di).wait_recv()
@@ -356,7 +402,22 @@
 
     stages = (chunk, step2, step3, step4, step5)
 
+    def weights_in(c):
+        if c <= 5:
+            pump(14 + c)
+        if c < 7:
+            hop = (c + 1) // 2
+            pwait(2, (2 * hop - 2, 2 * hop - 1), ((c + 1) % 2,))
+        if c == 6:
+            pump(20)
+        if c == 7:
+            pwait(2, (6,))
+
     def turn(i, carry):
+        for c in range(1, 8):
+            @pl.when(i == c)
+            def _(c=c):
+                weights_in(c)
         for j, fn in enumerate(stages):
             @pl.when((i >= j) & (i < NZ + j))
             def _(j=j, fn=fn):
@@ -367,8 +428,7 @@
 
     final = pltpu.make_async_copy(outv, out_ref, osem)
     final.start()
-    for c in sends:
-        c.wait_send()
+    zdrain()
 
     def drain(c, carry):
         for step in range(4):
@@ -380,20 +440,21 @@
 
 
 def layer(tokens, expert_ids, gate_weights, hot_ids, w_gate, w_up, w_down):
-    meta = jnp.concatenate([expert_ids.astype(F32), gate_weights], axis=1).T
     dma = pltpu.SemaphoreType.DMA
     any_spec = pl.BlockSpec(memory_space=pl.ANY)
     return pl.pallas_call(
         kernel,
         out_shape=jax.ShapeDtypeStruct((128, 2048), BF16),
-        in_specs=[any_spec] * 5,
+        in_specs=[any_spec] * 6,
         out_specs=any_spec,
         scratch_shapes=[
             pltpu.VMEM((4, 4, 128, 2048), BF16),
             pltpu.VMEM((4, 4, 8, 128), F32),
+            pltpu.VMEM((4, 128), jnp.int32),
+            pltpu.VMEM((4, 128), F32),
             pltpu.VMEM((2, 2048, 1536), BF16),
             pltpu.VMEM((8, 2, 768, 256), BF16),
-            pltpu.VMEM((2, 1024, 2048), BF16),
+            pltpu.VMEM((1024, 1536), F32),
             pltpu.VMEM((2, 1024, 768), BF16),
             pltpu.VMEM((2, 1024, 1), F32),
             pltpu.VMEM((16, 128, 128), BF16),
@@ -404,7 +465,7 @@
             pltpu.VMEM((8, 2, 2, 64, 128), BF16),
             pltpu.VMEM((8, 2, 2, 128, 128), BF16),
             pltpu.VMEM((128, 2048), BF16),
-            dma((8,)),
+            dma((9,)),
             dma((2, 21)), dma((2, 21)),
             dma((3, 16)), dma((3, 16)),
             dma((4, 2, 2)), dma((4, 2, 2)),
@@ -415,7 +476,7 @@
         compiler_params=pltpu.CompilerParams(
             collective_id=0, has_side_effects=True, vmem_limit_bytes=67043328
         ),
-    )(tokens, meta, w_gate, w_up, w_down)
+    )(tokens, expert_ids.T, gate_weights.T, w_gate, w_up, w_down)
 
 
 def solution(mesh):

time: 162 us -> 141 us (0.87)
  Pallas kernels: 158 us -> 139 us
    pallas_call x1, Pallas kernels: 158 us -> 139 us  [layer(): pl.pallas_call(kernel, out_shape=jax.ShapeDtypeStruct((128, 2048), BF16),...]
where the time goes in v2:
time: 141 us
  Pallas kernels  139 us (99%)
  local copies, waits for them, and re-layouts  1.88 us (1%)
    pallas_call x1, Pallas kernels, layer(): pl.pallas_call(kernel, out_shape=jax.ShapeDtypeStruct((128, 2048), BF16),...  139 us

profile of v2, /device:TPU:1, one launch (start us, length us, event | category | flops | bytes accessed | tf_op | source)
XLA Modules:
  0.0 141.3 jit_solution(5946347243090821205)
XLA Ops:
  0.0 139.4 %shard_map.64 = bf16[128,2048]{1,0:T(8,128)(2,1)} custom-call(bf16[128,2048]{1,0:T(8,128)(2,1)} %tok_in.1, s32[4,128]{1,0:T(4,128)} %bitcast.2, f32[4,128]{1,0:T(4,128)} %bitcast.3, bf16[2,128,768]{2,1,0:T(8,128)(2,1)} %wg_in.1, bf16[2,128,768]{2,1,0:T(8,128)(2,1)} %wu_in.1, bf16[2,768,128]{2,1,0:T(8,128)(2,1)} %wd_in.1), custom_call_target="tpu_custom_call" | custom-call | tf_op jit(solution)/shard_map/pallas_call | solution.py:445
  139.4 1.9 %copy.8 = bf16[128,2048]{1,0:T(8,128)(2,1)} copy(bf16[128,2048]{1,0:T(8,128)(2,1)} %shard_map.64) | data formatting | bytes 1048576

commit v3 on v2

--- a/solution.py
+++ b/solution.py
@@ -10,6 +10,9 @@
 SIDE = 4
 SLOTS = 64
 DIRS = (1, -1)
+NEAR = ((0, 0), (1, 0), (-1, 0), (0, 1), (0, -1), (1, 1), (1, -1), (-1, 1))
+FAR = ((-1, -1), (2, 0), (2, 1), (2, -1), (0, 2), (1, 2), (-1, 2), (2, 2))
+SOURCES = NEAR + FAR
 F32 = jnp.float32
 BF16 = jnp.bfloat16
 
@@ -226,10 +229,11 @@
         if n == 5:
             meta_step(4)
     tok_step(3)
-    for n in range(8, 10):
-        pump(n)
-
-    rows = meta[...].reshape(16, 8, 128)
+
+    def source(q):
+        return w4(x + SOURCES[q][0]), w4(y + SOURCES[q][1])
+
+    rows = jnp.stack([meta[source(q)] for q in range(16)])
     mine = [(ex * 2).astype(F32), (ex * 2 + 1).astype(F32)]
     hits, gates = [], []
     for e in range(2):
@@ -243,29 +247,22 @@
     slot = jnp.where(hit > 0.5, rank + lift, -1.0)
     slot_cols = jnp.transpose(jnp.concatenate([slot, jnp.zeros((96, 128), F32)], axis=0))
 
-    tok_step(4)
-    for c in sends:
-        c.wait_send()
     down_i = lax.broadcasted_iota(jnp.int32, (128, 128), 0).astype(F32)
     across_i = lax.broadcasted_iota(jnp.int32, (128, 128), 1).astype(F32)
-    for s in range(16):
-        pick = (slot[s:s + 1] == down_i) | (slot[16 + s:17 + s] == down_i)
-        gate_of = jnp.where(down_i < SLOTS, gates[0][s:s + 1], gates[1][s:s + 1])
-        g_col = jnp.sum(jnp.where(pick, gate_of, 0.0), axis=1, keepdims=True)
-        for e in range(2):
-            gs[e, pl.ds(s * SLOTS, SLOTS), :] = g_col[e * SLOTS:(e + 1) * SLOTS]
-        back = (slot_cols[:, s:s + 1] == across_i) | (slot_cols[:, 16 + s:17 + s] == across_i)
-        pt[s] = jnp.where(back, 1.0, 0.0).astype(BF16)
-        picked = jnp.where(pick, 1.0, 0.0).astype(BF16)
-        got = jnp.dot(picked, tok[s // SIDE, s % SIDE], preferred_element_type=F32)
-        tok[s // SIDE, s % SIDE] = got.astype(BF16)
-    pump(10)
-    pwait_own(0)
-    pwait(0, range(7))
-
-    def finish(e, gate, up, r0, c0):
-        h = gate / (1.0 + jnp.exp(-gate)) * up * gs[e, pl.ds(r0, 512), :]
-        hid[e, pl.ds(r0, 512), pl.ds(c0, 256)] = h.astype(BF16)
+
+    def gather(qs_):
+        for q in qs_:
+            pick = (slot[q:q + 1] == down_i) | (slot[16 + q:17 + q] == down_i)
+            gate_of = jnp.where(down_i < SLOTS, gates[0][q:q + 1], gates[1][q:q + 1])
+            g_col = jnp.sum(jnp.where(pick, gate_of, 0.0), axis=1, keepdims=True)
+            for e in range(2):
+                gs[e, pl.ds(q * SLOTS, SLOTS), :] = g_col[e * SLOTS:(e + 1) * SLOTS]
+            back = (slot_cols[:, q:q + 1] == across_i) | (slot_cols[:, 16 + q:17 + q] == across_i)
+            pt[q] = jnp.where(back, 1.0, 0.0).astype(BF16)
+            picked = jnp.where(pick, 1.0, 0.0).astype(BF16)
+            got = jnp.dot(picked, tok[source(q)], preferred_element_type=F32).astype(BF16)
+            for c in range(NZ):
+                part[c, q // SIDE, q % SIDE] = got[:, c * 256:(c + 1) * 256]
 
     def gate_up(e, offs, first, last, lo, hi):
         def body(i, carry):
@@ -273,44 +270,51 @@
             r0 = pl.multiple_of(mb * 512, 512)
             c0 = pl.multiple_of((i % 3) * 256, 256)
             c1 = pl.multiple_of(768 + (i % 3) * 256, 256)
-            who = (pl.ds(mb * 2, 2), slice(None), pl.ds(e * SLOTS, SLOTS))
-            sums = [None, None]
-            if offs is None:
-                rws = tok[who + (slice(None),)].reshape(512, 2048)
-                for j, c in enumerate((c0, c1)):
-                    sums[j] = jnp.dot(rws, wgu[e, :, pl.ds(c, 256)], preferred_element_type=F32)
+            deep = range(NZ) if offs is None else [(z + off + NZ) % NZ for off in offs]
+            rws = jnp.concatenate(
+                [part[c, pl.ds(mb * 2, 2), :, pl.ds(e * SLOTS, SLOTS), :].reshape(512, 256) for c in deep], axis=1
+            )
+            sums = []
+            for col in (c0, c1):
+                w = jnp.concatenate(
+                    [wgu[e, pl.ds(pl.multiple_of(c * 256, 256), 256), pl.ds(col, 256)] for c in deep], axis=0
+                )
+                total = jnp.dot(rws, w, preferred_element_type=F32)
+                sums.append(total if first else total + acc[pl.ds(r0, 512), pl.ds(col, 256)])
+            if last:
+                gate, up = sums
+                h = gate / (1.0 + jnp.exp(-gate)) * up * gs[e, pl.ds(r0, 512), :]
+                hid[e, pl.ds(r0, 512), pl.ds(c0, 256)] = h.astype(BF16)
             else:
-                for j, c in enumerate((c0, c1)):
-                    total = None if first else acc[pl.ds(r0, 512), pl.ds(c, 256)]
-                    for off in offs:
-                        deep = pl.ds(pl.multiple_of(((z + off + NZ) % NZ) * 256, 256), 256)
-                        rws = tok[who + (deep,)].reshape(512, 256)
-                        term = jnp.dot(rws, wgu[e, deep, pl.ds(c, 256)], preferred_element_type=F32)
-                        total = term if total is None else total + term
-                    sums[j] = total
-            if last:
-                finish(e, sums[0], sums[1], r0, c0)
-            else:
-                for j, c in enumerate((c0, c1)):
-                    acc[pl.ds(r0, 512), pl.ds(c, 256)] = sums[j]
+                for col, total in zip((c0, c1), sums):
+                    acc[pl.ds(r0, 512), pl.ds(col, 256)] = total
             return carry
 
         lax.fori_loop(lo, hi, body, 0)
 
-    gate_up(0, None, True, True, 0, 4)
+    soon = (0, -1, 1, -2, 2)
+    gather(range(8))
+    pwait_own(0)
+    pwait(0, range(7))
+    gate_up(0, None, True, True, 0, 2)
+    pump(8)
+    gate_up(0, None, True, True, 2, 3)
+    pump(9)
+    tok_step(4)
+    gather(range(8, 16))
+    pump(10)
+    gate_up(0, None, True, True, 3, 6)
     pump(11)
-    gate_up(0, None, True, True, 4, 6)
     pwait_own(1)
     pwait(1, range(4))
-    gate_up(1, (0, -1, 1, -2, 2), True, False, 0, 2)
+    gate_up(1, soon, True, False, 0, 4)
     pump(12)
-    gate_up(1, (0, -1, 1, -2, 2), True, False, 2, 6)
+    gate_up(1, soon, True, False, 4, 6)
     pwait(1, (4, 5))
     gate_up(1, (-3, 3), False, False, 0, 6)
     pump(13)
     pwait(1, (6,))
     gate_up(1, (4,), False, True, 0, 6)
-    pump(14)
     pwait_own(2)
 
     def cc(o):
@@ -356,12 +360,10 @@
             yv = jnp.dot(hid[e], wd[zz, e], preferred_element_type=F32).astype(BF16)
             ybuf[:, pl.ds(e * SLOTS, SLOTS), :] = yv.reshape(16, SLOTS, 256)
 
-        def scatter(s, carry):
-            v = jnp.dot(pt[s], ybuf[s], preferred_element_type=F32).astype(BF16)
-            part[c, s // SIDE, s % SIDE] = v
-            return carry
-
-        lax.fori_loop(0, 16, scatter, 0, unroll=4)
+        for q in range(16):
+            v = jnp.dot(pt[q], ybuf[q], preferred_element_type=F32).astype(BF16)
+            sx, sy = source(q)
+            part[c, sx, sy] = v
         both(lambda o, di: link(0, c, o, di).start())
 
     def step2(c):
@@ -400,9 +402,11 @@
             col = pl.multiple_of(zz * 256 + o * 128, 128)
             outv[:, pl.ds(col, 128)] = total.astype(BF16)
 
-    stages = (chunk, step2, step3, step4, step5)
+    stages = ((0, chunk), (1, step2), (3, step3), (5, step4), (7, step5))
 
     def weights_in(c):
+        if c == 1:
+            pump(14)
         if c <= 5:
             pump(14 + c)
         if c < 7:
@@ -418,16 +422,18 @@
             @pl.when(i == c)
             def _(c=c):
                 weights_in(c)
-        for j, fn in enumerate(stages):
+        for j, fn in stages:
             @pl.when((i >= j) & (i < NZ + j))
             def _(j=j, fn=fn):
                 fn(i - j)
         return carry
 
-    lax.fori_loop(0, NZ + len(stages) - 1, turn, 0)
+    lax.fori_loop(0, NZ + stages[-1][0], turn, 0)
 
     final = pltpu.make_async_copy(outv, out_ref, osem)
     final.start()
+    for c in sends:
+        c.wait_send()
     zdrain()
 
     def drain(c, carry):

time: 141 us -> 137 us (0.972)
  Pallas kernels: 139 us -> 134 us
    pallas_call x1, Pallas kernels: 139 us -> 134 us  [layer(): pl.pallas_call(kernel, out_shape=jax.ShapeDtypeStruct((128, 2048), BF16),...]
where the time goes in v3:
time: 137 us; the launch traced here: 136 us
  Pallas kernels  134 us (98%)
  local copies, waits for them, and re-layouts  1.88 us (1%)
    pallas_call x1, Pallas kernels, layer(): pl.pallas_call(kernel, out_shape=jax.ShapeDtypeStruct((128, 2048), BF16),...  134 us

profile of v3, /device:TPU:1, one launch (start us, length us, event | category | flops | bytes accessed | tf_op | source)
XLA Modules:
  0.0 136.0 jit_solution(3036776173750676954)
XLA Ops:
  0.0 134.1 %shard_map.64 = bf16[128,2048]{1,0:T(8,128)(2,1)} custom-call(bf16[128,2048]{1,0:T(8,128)(2,1)} %tok_in.1, s32[4,128]{1,0:T(4,128)} %bitcast.2, f32[4,128]{1,0:T(4,128)} %bitcast.3, bf16[2,128,768]{2,1,0:T(8,128)(2,1)} %wg_in.1, bf16[2,128,768]{2,1,0:T(8,128)(2,1)} %wu_in.1, bf16[2,768,128]{2,1,0:T(8,128)(2,1)} %wd_in.1), custom_call_target="tpu_custom_call" | custom-call | tf_op jit(solution)/shard_map/pallas_call | solution.py:451
  134.1 1.9 %copy.8 = bf16[128,2048]{1,0:T(8,128)(2,1)} copy(bf16[128,2048]{1,0:T(8,128)(2,1)} %shard_map.64) | data formatting | bytes 1048576

commit v4 on v3

--- a/solution.py
+++ b/solution.py
@@ -360,11 +360,18 @@
             yv = jnp.dot(hid[e], wd[zz, e], preferred_element_type=F32).astype(BF16)
             ybuf[:, pl.ds(e * SLOTS, SLOTS), :] = yv.reshape(16, SLOTS, 256)
 
-        for q in range(16):
+        def scatter(q):
             v = jnp.dot(pt[q], ybuf[q], preferred_element_type=F32).astype(BF16)
             sx, sy = source(q)
             part[c, sx, sy] = v
+
+        across = [q for q in range(16) if 2 in SOURCES[q]]
+        for q in across:
+            scatter(q)
         both(lambda o, di: link(0, c, o, di).start())
+        for q in range(16):
+            if q not in across:
+                scatter(q)
 
     def step2(c):
         def one(o, di):
@@ -391,6 +398,10 @@
             link(3, c, o, di).start()
 
         both(one)
+
+    def result(c):
+        cols = pl.ds(pl.multiple_of(origin(c) * 256, 256), 256)
+        return pltpu.make_async_copy(outv.at[:, cols], out_ref.at[:, cols], osem.at[c])
 
     def step5(c):
         zz = origin(c)
@@ -401,6 +412,9 @@
             total = qblk(o, c, n, every)[...].astype(F32) + r4[c, o, 0].astype(F32) + r4[c, o, 1].astype(F32)
             col = pl.multiple_of(zz * 256 + o * 128, 128)
             outv[:, pl.ds(col, 128)] = total.astype(BF16)
+        result(c).start()
+        for step in range(4):
+            both(lambda o, di: link(step, c, o, di).wait_send())
 
     stages = ((0, chunk), (1, step2), (3, step3), (5, step4), (7, step5))
 
@@ -426,23 +440,22 @@
             @pl.when((i >= j) & (i < NZ + j))
             def _(j=j, fn=fn):
                 fn(i - j)
+
+        @pl.when(i == 10)
+        def _():
+            for c in sends:
+                c.wait_send()
+            zdrain()
+
         return carry
 
     lax.fori_loop(0, NZ + stages[-1][0], turn, 0)
 
-    final = pltpu.make_async_copy(outv, out_ref, osem)
-    final.start()
-    for c in sends:
-        c.wait_send()
-    zdrain()
-
-    def drain(c, carry):
-        for step in range(4):
-            both(lambda o, di: link(step, c, o, di).wait_send())
+    def finish(c, carry):
+        result(c).wait()
         return carry
 
-    lax.fori_loop(0, NZ, drain, 0)
-    final.wait()
+    lax.fori_loop(0, NZ, finish, 0)
 
 
 def layer(tokens, expert_ids, gate_weights, hot_ids, w_gate, w_up, w_down):
@@ -477,7 +490,7 @@
             dma((4, 2, 2)), dma((4, 2, 2)),
             dma((6,)), dma((6,)),
             dma((4, 8, 2, 2)), dma((4, 8, 2, 2)),
-            dma,
+            dma((8,)),
         ],
         compiler_params=pltpu.CompilerParams(
             collective_id=0, has_side_effects=True, vmem_limit_bytes=67043328

time: 137 us -> 137 us (level)
  no operation moved by 1% of the time
where the time goes in v4:
time: 137 us; the launch traced here: 136 us
  Pallas kernels  134 us (98%)
  local copies, waits for them, and re-layouts  1.88 us (1%)
    pallas_call x1, Pallas kernels, layer(): pl.pallas_call(kernel, out_shape=jax.ShapeDtypeStruct((128, 2048), BF16),...  134 us

profile of v4, /device:TPU:1, one launch (start us, length us, event | category | flops | bytes accessed | tf_op | source)
XLA Modules:
  0.0 135.8 jit_solution(16281896947284315505)
XLA Ops:
  0.0 133.9 %shard_map.64 = bf16[128,2048]{1,0:T(8,128)(2,1)} custom-call(bf16[128,2048]{1,0:T(8,128)(2,1)} %tok_in.1, s32[4,128]{1,0:T(4,128)} %bitcast.2, f32[4,128]{1,0:T(4,128)} %bitcast.3, bf16[2,128,768]{2,1,0:T(8,128)(2,1)} %wg_in.1, bf16[2,128,768]{2,1,0:T(8,128)(2,1)} %wu_in.1, bf16[2,768,128]{2,1,0:T(8,128)(2,1)} %wd_in.1), custom_call_target="tpu_custom_call" | custom-call | tf_op jit(solution)/shard_map/pallas_call | solution.py:464
  133.9 1.9 %copy.8 = bf16[128,2048]{1,0:T(8,128)(2,1)} copy(bf16[128,2048]{1,0:T(8,128)(2,1)} %shard_map.64) | data formatting | bytes 1048576

commit v5 on v4

--- a/solution.py
+++ b/solution.py
@@ -283,7 +283,8 @@
                 sums.append(total if first else total + acc[pl.ds(r0, 512), pl.ds(col, 256)])
             if last:
                 gate, up = sums
-                h = gate / (1.0 + jnp.exp(-gate)) * up * gs[e, pl.ds(r0, 512), :]
+                half = 0.5 * gate
+                h = (half + half * jnp.tanh(half)) * up * gs[e, pl.ds(r0, 512), :]
                 hid[e, pl.ds(r0, 512), pl.ds(c0, 256)] = h.astype(BF16)
             else:
                 for col, total in zip((c0, c1), sums):

time: 137 us -> 137 us (level)
  no operation moved by 1% of the time
where the time goes in v5:
time: 137 us; the launch traced here: 136 us
  Pallas kernels  134 us (98%)
  local copies, waits for them, and re-layouts  1.88 us (1%)
    pallas_call x1, Pallas kernels, layer(): pl.pallas_call(kernel, out_shape=jax.ShapeDtypeStruct((128, 2048), BF16),...  134 us

profile of v5, /device:TPU:1, one launch (start us, length us, event | category | flops | bytes accessed | tf_op | source)
XLA Modules:
  0.0 135.8 jit_solution(3177464460763720948)
XLA Ops:
  0.0 133.9 %shard_map.64 = bf16[128,2048]{1,0:T(8,128)(2,1)} custom-call(bf16[128,2048]{1,0:T(8,128)(2,1)} %tok_in.1, s32[4,128]{1,0:T(4,128)} %bitcast.2, f32[4,128]{1,0:T(4,128)} %bitcast.3, bf16[2,128,768]{2,1,0:T(8,128)(2,1)} %wg_in.1, bf16[2,128,768]{2,1,0:T(8,128)(2,1)} %wu_in.1, bf16[2,768,128]{2,1,0:T(8,128)(2,1)} %wd_in.1), custom_call_target="tpu_custom_call" | custom-call | tf_op jit(solution)/shard_map/pallas_call | solution.py:465
  133.9 1.9 %copy.8 = bf16[128,2048]{1,0:T(8,128)(2,1)} copy(bf16[128,2048]{1,0:T(8,128)(2,1)} %shard_map.64) | data formatting | bytes 1048576
